TPU v7x, 512 devices: a whole 4x4x16 slice. The times are simulated.
512 devices in a mesh: seq: 32 (over x, y, core), tensor: 16 (over z).
Axes of the slice: x: 4, y: 4, z: 16, core: 2. Of those that a mesh axis runs over, the one named last changes fastest.
Arguments:
- byte_states: bfloat16 [32768, 1024], P('seq'), may hold values from -6 to 6
- byte_patch: int32 [32768], P('seq'), may hold values from 0 to 4095, as said below
- patch_len: int32 [4096], replicated, may hold values from 1 to 1024, as said below
- cross_query: bfloat16 [1024, 4096], P('seq', 'tensor'), may hold values from -0.75 to 0.75
- cross_key: bfloat16 [1024, 4096], P('seq', 'tensor'), may hold values from -0.375 to 0.375
- cross_value: bfloat16 [1024, 4096], P('seq', 'tensor'), may hold values from -0.1875 to 0.1875
- cross_out: bfloat16 [4096, 4096], P('tensor', 'seq'), may hold values from -0.09375 to 0.09375
- norm_gain: float32 [4096], replicated, may hold values from 0.5 to 1.5
- latent_query: bfloat16 [4096, 4096], P('seq', 'tensor'), may hold values from -0.1875 to 0.1875
- latent_key: bfloat16 [4096, 4096], P('seq', 'tensor'), may hold values from -0.1875 to 0.1875
- latent_value: bfloat16 [4096, 4096], P('seq', 'tensor'), may hold values from -0.09375 to 0.09375
- latent_out: bfloat16 [4096, 4096], P('tensor', 'seq'), may hold values from -0.09375 to 0.09375
Outputs:
- patch_latent: bfloat16 [4096, 4096], P('seq', 'tensor')
Inputs may be any that keep to these rules, and one draw needn't show every extreme that they name: `byte_patch`: within each aligned block of 1024 bytes the numbers never fall and rise by at most one from byte to byte, and the block's first byte starts a new patch, so no patch spans two blocks. Block k begins with patch number k * 128 + r with -64 <= r < 64; the first block begins with 0 and the last ends with 4095. A block holds 1 to 255 patches; some block holds exactly 255 and the block after it exactly one. patch_len[p] is the number of bytes b with byte_patch[b] = p.
All inputs are finite; a program needn't handle non-finite values.
Results may differ from a plain program's by a relative error of at most 0.028.
Values may be sent and summed in bfloat16 or wider, within the bound.
A program may use at most 64 MiB of HBM per device.

v0:
```python
import math

import jax
import jax.numpy as jnp
from jax import lax
from jax.sharding import PartitionSpec as P

HEAD_DIM = 128
PATCH_DEV = 128


score_cap = 30.0
norm_eps = 1e-05


def side_by_side(arrays, axis, dim, along):
    widths = [a.shape[along] for a in arrays]
    both = jnp.concatenate(arrays, axis=along)
    result = lax.all_gather(both, axis, axis=dim, tiled=True)
    return tuple(jnp.split(result, [sum(widths[:k]) for k in range(1, len(widths))], axis=along))


def shifted(block, axis, distance):
    devices = range(lax.axis_size(axis))
    route = [(i - distance, i) for i in devices if i - distance in devices]
    return lax.ppermute(block, axis, route)


def capped_exp(scores):
    return jnp.exp(score_cap * jnp.tanh(scores / score_cap))


def contract_rows(left, right):
    return lax.dot_general(
        left,
        right,
        (((0,), (0,)), ((), ())),
        precision=lax.Precision.HIGHEST,
        preferred_element_type=jnp.float32,
    )


def per_device(
    byte_states,
    byte_patch,
    patch_len,
    cross_query,
    cross_key,
    cross_value,
    cross_out,
    norm_gain,
    latent_query,
    latent_key,
    latent_value,
    latent_out,
):
    seq_index = lax.axis_index("seq")
    tensor_count = lax.axis_size("tensor")
    (
        cross_query,
        cross_key,
        cross_value,
        latent_query,
        latent_key,
        latent_value,
        cross_out,
        latent_out,
    ) = (
        *side_by_side((cross_query, cross_key, cross_value), "seq", 0, 1),
        *side_by_side((latent_query, latent_key, latent_value), "seq", 0, 1),
        *side_by_side((cross_out, latent_out), "seq", 1, 0),
    )
    latent_width = cross_out.shape[1]
    local_width = cross_out.shape[0]
    head_count = local_width // HEAD_DIM
    slot_count = 2 * PATCH_DEV
    byte_count = byte_states.shape[0]
    first_patch = byte_patch[0]
    slot_of = byte_patch - first_patch
    onehot_mask = slot_of[:, None] == jnp.arange(slot_count, dtype=jnp.int32)[None, :]
    onehot = onehot_mask.astype(jnp.bfloat16)
    onehot_float = onehot_mask.astype(jnp.float32)
    byte_sums = lax.dot_general(
        onehot, byte_states, (((0,), (0,)), ((), ())), preferred_element_type=jnp.float32
    )
    lengths_all = jnp.concatenate([patch_len, jnp.ones((slot_count,), jnp.int32)])
    lengths = lax.dynamic_slice_in_dim(lengths_all, first_patch, slot_count)
    pooled = (byte_sums / lengths.astype(jnp.float32)[:, None]).astype(jnp.bfloat16)
    query_slots = jnp.dot(pooled, cross_query, preferred_element_type=jnp.float32).astype(
        jnp.bfloat16
    )
    byte_keys = jnp.dot(byte_states, cross_key, preferred_element_type=jnp.float32).astype(
        jnp.bfloat16
    )
    byte_values = jnp.dot(byte_states, cross_value, preferred_element_type=jnp.float32).astype(
        jnp.bfloat16
    )
    query_bytes = jnp.dot(onehot, query_slots, preferred_element_type=jnp.float32)
    scores = (query_bytes * byte_keys.astype(jnp.float32)).reshape(
        byte_count, head_count, HEAD_DIM
    ).sum(axis=2) / math.sqrt(HEAD_DIM)
    byte_raw = capped_exp(scores)
    totals = contract_rows(onehot_float, byte_raw)
    totals = jnp.where(totals > 0.0, totals, 1.0)
    totals_bytes = jnp.dot(
        onehot_float, totals, precision=lax.Precision.HIGHEST, preferred_element_type=jnp.float32
    )
    byte_weight = (byte_raw / totals_bytes).astype(jnp.bfloat16)
    weighted = (
        byte_weight.astype(jnp.float32)[:, :, None]
        * byte_values.astype(jnp.float32).reshape(byte_count, head_count, HEAD_DIM)
    ).reshape(byte_count, local_width)
    cross_heads = contract_rows(onehot_float, weighted).astype(jnp.bfloat16)
    padding = jnp.zeros((2 * PATCH_DEV, cross_heads.shape[1]), cross_heads.dtype)
    padded = jnp.concatenate([padding, cross_heads, padding], axis=0)
    offset = seq_index * PATCH_DEV - first_patch + 2 * PATCH_DEV
    padded, offset = (padded, offset)
    owned_heads = lax.dynamic_slice_in_dim(padded, offset, PATCH_DEV, 0)
    for offset_step in (-1, 1):
        window = lax.dynamic_slice_in_dim(padded, offset + offset_step * PATCH_DEV, PATCH_DEV, 0)
        owned_heads = owned_heads + shifted(window, "seq", offset_step)
    partial_value = jnp.dot(owned_heads, cross_out, preferred_element_type=jnp.float32)
    latent_in = lax.psum(partial_value, "tensor").astype(jnp.bfloat16)
    hidden = latent_in.astype(jnp.float32)
    mean_square = jnp.mean(hidden * hidden, axis=1, keepdims=True)
    normed = (hidden * lax.rsqrt(mean_square + norm_eps) * norm_gain[None, :]).astype(jnp.bfloat16)
    query = (
        jnp.dot(normed, latent_query, preferred_element_type=jnp.float32)
        .astype(jnp.bfloat16)
        .reshape(PATCH_DEV, head_count, HEAD_DIM)
    )
    key_rows = jnp.dot(normed, latent_key, preferred_element_type=jnp.float32).astype(jnp.bfloat16)
    value_rows = jnp.dot(normed, latent_value, preferred_element_type=jnp.float32).astype(
        jnp.bfloat16
    )
    positions = seq_index * PATCH_DEV + jnp.arange(PATCH_DEV, dtype=jnp.int32)
    key_piece, value_piece = side_by_side((key_rows, value_rows), "seq", 0, 1)
    piece_rows = key_piece.shape[0]
    key_piece = key_piece.reshape(piece_rows, head_count, HEAD_DIM)
    value_piece = value_piece.reshape(piece_rows, head_count, HEAD_DIM)
    piece_scores = jnp.einsum(
        "qhd,khd->hqk", query, key_piece, preferred_element_type=jnp.float32
    ) / math.sqrt(HEAD_DIM)
    key_positions = jnp.arange(piece_rows, dtype=jnp.int32)
    allowed = key_positions[None, :] <= positions[:, None]
    exp_scores = jnp.where(allowed[None, :, :], capped_exp(piece_scores), 0.0)
    denominator = jnp.sum(exp_scores, axis=2)
    numerator = jnp.einsum(
        "hqk,khd->hqd",
        exp_scores.astype(jnp.bfloat16),
        value_piece,
        preferred_element_type=jnp.float32,
    )
    numerator, denominator = (numerator, denominator)
    attended = (numerator / denominator[:, :, None]).astype(jnp.bfloat16)
    attended = attended.transpose(1, 0, 2).reshape(PATCH_DEV, local_width)
    projected = jnp.dot(attended, latent_out, preferred_element_type=jnp.float32)
    mixed_sum = lax.psum_scatter(projected, "tensor", scatter_dimension=1, tiled=True)
    column_width = latent_width // tensor_count
    residual = lax.dynamic_slice_in_dim(
        hidden, lax.axis_index("tensor") * column_width, column_width, 1
    )
    return (residual + mixed_sum).astype(jnp.bfloat16)


def solution(mesh):
    return jax.shard_map(
        per_device,
        mesh=mesh,
        in_specs=(
            P("seq", None),
            P("seq"),
            P(),
            P("seq", "tensor"),
            P("seq", "tensor"),
            P("seq", "tensor"),
            P("tensor", "seq"),
            P(),
            P("seq", "tensor"),
            P("seq", "tensor"),
            P("seq", "tensor"),
            P("tensor", "seq"),
        ),
        out_specs=P("seq", "tensor"),
        check_vma=False,
    )
```

profile of v0, /device:TPU:4, one launch (start us, length us, event | category | flops | bytes accessed | tf_op | source)
XLA Modules:
  0.0 380.0 jit_solution(9629683256341763754)
XLA Ops:
  6.5 1.5 pad_maximum_fusion.4
  8.1 1.5 pad_maximum_fusion.2
  9.7 1.6 pad_maximum_fusion.1
  11.4 1.2 slice.3
  14.9 0.8 fusion.66
  15.6 1.2 broadcast_subtract_fusion
  16.9 55.9 %all-gather.5.cloned.1.call-done = bf16[1024,768]{1,0:T(8,128)(2,1)} async-done(((bf16[32,768]{1,0:T(8,128)(2,1)}), bf16[1024,768]{1,0:T(8,128)(2,1)}) %all-gather.5.cloned.1.call-update) | async-done | bytes 1572880 | tf_op jit(solution)/shard_map/all_gather | solution.py:19
  72.8 1.8 fusion.20
  74.6 2.2 fusion.25
  78.7 1.2 mul.48
  79.9 1.8 fusion.23
  81.7 1.2 convolution_convert_fusion.2
  83.0 3.2 collective-permute-start
  86.2 1.9 collective-permute-start.1
  88.1 5.7 %collective-permute-done.1 = bf16[128,256]{1,0:T(8,128)(2,1)S(1)} collective-permute-done((bf16[128,256]{1,0:T(8,128)(2,1)S(1)}, bf16[128,256]{1,0:T(8,128)(2,1)S(1)}, u32[]{:S(2)}, u32[]{:S(2)}) %collective-permute-start.1) | collective-permute-done | bytes 65568 | tf_op jit(solution)/shard_map/ppermute | solution.py:26
  93.9 44.3 %all-gather.7.cloned.1.call-done = bf16[512,4096]{1,0:T(8,128)(2,1)} async-done(((bf16[512,128]{1,0:T(8,128)(2,1)}), bf16[512,4096]{1,0:T(8,128)(2,1)}) %all-gather.7.cloned.1.call-update) | async-done | bytes 4194320 | tf_op jit(solution)/shard_map/all_gather | solution.py:19
  138.2 3.4 fusion.14
  141.6 76.8 %all-reduce.2 = bf16[128,4096]{1,0:T(8,128)(2,1)S(1)} all-reduce(f32[128,4096]{1,0:T(8,128)} %fusion.14), channel_id=1, replica_groups=mesh['seq'=32,'tensor'=16] {'tensor'}, use_global_device_ids=true, to_apply=%region_1.2 | all-reduce | flops 524288 | bytes 3145728 | tf_op jit(solution)/shard_map/psum | solution.py:123
  218.7 2.1 fusion.35
  220.8 2.1 fusion.38
  223.8 1.2 iota_compare_fusion
  225.0 2.1 fusion.44
  227.1 53.9 %all-gather.11.cloned.1.call-done = bf16[4096,512]{1,0:T(8,128)(2,1)} async-done(((bf16[128,512]{1,0:T(8,128)(2,1)}), bf16[4096,512]{1,0:T(8,128)(2,1)}) %all-gather.11.cloned.1.call-update) | async-done | bytes 4194320 | tf_op jit(solution)/shard_map/all_gather | solution.py:19
  281.0 4.6 %slice_bitcast_fusion = (bf16[512,2,8,128]{3,2,1,0:T(8,128)(2,1)}, bf16[4096,256]{1,0:T(8,128)(2,1)}) fusion(bf16[4096,512]{1,0:T(8,128)(2,1)} %all-gather.11.cloned.1.call-done), kind=kLoop, calls=%fused_computation.9 | loop fusion | bytes 8388608
  285.7 4.1 %copy.17 = bf16[4096,256]{0,1:T(8,128)(2,1)} copy(bf16[4096,256]{1,0:T(8,128)(2,1)} %get-tuple-element.6) | data formatting | bytes 4194304 | tf_op jit(solution)/shard_map/reshape | solution.py:140
  289.7 3.6 fusion.69
  293.4 0.7 fusion.41
  294.1 1.5 copy-done.1
  295.5 1.8 fusion.6
  297.4 1.5 convert_element_type.145
  298.9 73.0 %reduce-scatter.2.cloned.1.call-done = f32[128,256]{1,0:T(8,128)} async-done(((f32[128,4096]{1,0:T(8,128)}), f32[128,256]{1,0:T(8,128)}) %reduce-scatter.2.cloned.1.call-update) | async-done | bytes 131088 | tf_op jit(solution)/shard_map/reduce_scatter | solution.py:158
  371.9 1.6 add_convert_fusion
  (30 shorter events, 3.4 us)
Async XLA Ops:
  6.5 66.3 %copy-start = (bf16[1024,1024]{1,0:T(8,128)(2,1)S(1)}, bf16[1024,1024]{1,0:T(8,128)(2,1)}, u32[]{:S(2)}) copy-start(bf16[1024,1024]{1,0:T(8,128)(2,1)} %param.12) | copy-start | bytes 6291460
  6.5 66.3 %all-gather.5.cloned.1.call-start = ((), (), s32[]{:S(2)}) async-start(), calls=%async_computation.1 | async-start | bytes 1622016 | tf_op jit(solution)/shard_map/all_gather | solution.py:19
  8.1 130.1 %all-gather.7.cloned.1.call-start = ((), (), s32[]{:S(2)}) async-start(), calls=%async_computation.2 | async-start | bytes 4325376 | tf_op jit(solution)/shard_map/all_gather | solution.py:19
  9.7 209.0 %all-gather.9.cloned.1.call-start = ((), (), s32[]{:S(2)}) async-start(), calls=%async_computation.3 | async-start | bytes 6488064 | tf_op jit(solution)/shard_map/all_gather | solution.py:19
  11.4 269.7 %all-gather.11.cloned.1.call-start = ((), (), s32[]{:S(2)}) async-start(), calls=%async_computation.4 | async-start | bytes 4325376 | tf_op jit(solution)/shard_map/all_gather | solution.py:19
  83.0 5.2 %collective-permute-start = (bf16[128,256]{1,0:T(8,128)(2,1)S(1)}, bf16[128,256]{1,0:T(8,128)(2,1)S(1)}, u32[]{:S(2)}, u32[]{:S(2)}) collective-permute-start(bf16[128,256]{1,0:T(8,128)(2,1)S(1)} %get-tuple-element.7), channel_id=1, source_target_pairs={{16,0},{32,16},{48,32},{64,48},{80,64},{96,80},{112,96},{128,112},... | collective-permute-start | bytes 196616 | tf_op jit(solution)/shard_map/ppermute | solution.py:26
  86.2 7.7 %collective-permute-start.1 = (bf16[128,256]{1,0:T(8,128)(2,1)S(1)}, bf16[128,256]{1,0:T(8,128)(2,1)S(1)}, u32[]{:S(2)}, u32[]{:S(2)}) collective-permute-start(bf16[128,256]{1,0:T(8,128)(2,1)S(1)} %get-tuple-element.8), channel_id=1, source_target_pairs={{0,16},{16,32},{32,48},{48,64},{64,80},{80,96},{96,112},{112,128},... | collective-permute-start | bytes 196616 | tf_op jit(solution)/shard_map/ppermute | solution.py:26
  141.6 77.1 %copy-start.3 = (f32[4096]{0:T(1024)S(1)}, f32[4096]{0:T(1024)}, u32[]{:S(2)}) copy-start(f32[4096]{0:T(1024)} %param.19) | copy-start | bytes 49156
  223.6 148.3 %reduce-scatter.2.cloned.1.call-start = ((), (), s32[]{:S(2)}) async-start(), calls=%async_computation.5 | async-start | bytes 2228224 | tf_op jit(solution)/shard_map/reduce_scatter | solution.py:158
  289.7 3.6 copy-start.2
  293.3 2.2 copy-start.1
Sparse Core Ops, SparseCore 0:
  10.5 62.2 all-gather.4
  75.8 62.3 all-gather.6
  141.4 64.1 all-gather.8
  223.7 57.2 all-gather.10
  297.5 74.3 reduce-scatter.1
where the time goes:
time: 381 us; the launch traced here: 380 us
  waiting for transfers between devices  233 us (61%)
  blocking collectives  76.8 us (20%)
  matrix products  24.3 us (6%)
  between operations  15.6 us (4%)
  local copies, waits for them, and re-layouts  12.9 us (3%)
  other arithmetic  12 us (3%)
  starting transfers between devices  5.49 us (1%)
    all_gather x4, waiting for transfers between devices, side_by_side(): result = lax.all_gather(both, axis, axis=dim, tiled=True)  154 us
    psum x1, blocking collectives, per_device(): latent_in = lax.psum(partial_value, 'tensor').astype(jnp.bfloat16)  76.8 us
    reduce_scatter x1, waiting for transfers between devices, per_device(): lax.psum_scatter(projected, 'tensor', scatter_dimension=1, tiled=True)  73 us
  transfers between devices with their start and end apart: 7, of which 5 were waited for; matrix products, arithmetic and copies ran while one was open for 7% of the time, Pallas kernels for 0%

commit v1 on v0

v1 whole, which is shorter than its diff:
```python
import math

import jax
import jax.numpy as jnp
from jax import lax
from jax.experimental import pallas as pl
from jax.experimental.pallas import tpu as pltpu
from jax.sharding import PartitionSpec as P

MESH = pl.DeviceIdType.MESH
HEAD_DIM = 128
SIDE = 4
DEPTH = 16
ROWS = 256
CAP = 30.0
EPS = 1e-05
TEMPER = 1.0 / (CAP * math.sqrt(HEAD_DIM))
BF = jnp.bfloat16
F32 = jnp.float32

CROSS, OUT1, LATENT, OUT2 = (0, 96), (96, 128), (224, 384), (608, 128)
GROUPS = (CROSS, OUT1, LATENT, OUT2, (0, ROWS))
PACKED = 736
UP = DEPTH // 2
DOWN = DEPTH - 1 - UP


def dot(a, b):
    return jnp.dot(a, b, preferred_element_type=F32)


def dot_t(a, b):
    return lax.dot_general(a, b, (((1,), (1,)), ((), ())), preferred_element_type=F32)


def capped(raw):
    return jnp.exp(CAP * jnp.tanh(raw * TEMPER))


def kernel(
    bs_hbm, bp_ref, cq, ck, cv, co, gain, lq, lk, lv, lo,
    out_ref,
    bs, wp, wx, wf, pooled, kk, vv, wbuf, e1b, xbuf, rsend, rrecv, ag, acc, sq, e2, qs, kvb, oacc, lacc, att, latent, fin_s, fin_r,
    bs_sem, p1s, p1r, p2s, p2r, rls, rlr, rss, rsr, ags, agr, es, er,
):
    seq, z = lax.axis_index("seq"), lax.axis_index("tensor")
    k, c = lax.rem(seq, 2), lax.div(seq, 2)
    x, y = lax.div(c, SIDE), lax.rem(c, SIDE)
    started = []

    def wrap(i, n):
        return lax.rem(i + n, n)

    def dev(px, py, core, depth):
        return ((px * SIDE + py) * 2 + core, depth)

    def remote(src, dst, ssem, rsem, target):
        return pltpu.make_async_remote_copy(
            src_ref=src, dst_ref=dst, send_sem=ssem, recv_sem=rsem, device_id=target, device_id_type=MESH
        )

    def send(src, dst, ssem, rsem, target):
        copy = remote(src, dst, ssem, rsem, target)
        copy.start()
        started.append(copy)

    def arrive(dst, ssem, rsem):
        remote(dst, dst, ssem, rsem, partner).wait_recv()

    partner = (seq + 1 - 2 * k, z)
    up, down = (seq, wrap(z + 1, DEPTH)), (seq, wrap(z - 1, DEPTH))

    def along(half, phase, d):
        if (half == 0) == (phase == 1):
            return dev(wrap(x + d, SIDE), y, k, z)
        return dev(x, wrap(y + d, SIDE), k, z)

    def piece(buf, half, phase, d, r, n):
        part = pl.ds(r, n)
        if half == 0:
            return buf.at[wrap(x + d, SIDE), y, part, :] if phase == 1 else buf.at[:, wrap(y + d, SIDE), part, :]
        return buf.at[x, wrap(y + d, SIDE), part, :] if phase == 1 else buf.at[wrap(x + d, SIDE), :, part, :]

    def span(g, half):
        r, n = GROUPS[g]
        return r + half * (n // 2), n // 2

    def phase_start(buf, g, phase, steps):
        ssem, rsem = (p1s, p1r) if phase == 1 else (p2s, p2r)
        for half in range(2):
            own = piece(buf, half, phase, 0, *span(g, half))
            for d in steps:
                send(own, own, ssem.at[g, half, d - 1], rsem.at[g, half, d - 1], along(half, phase, d))

    def phase_wait(buf, g, phase, steps):
        ssem, rsem = (p1s, p1r) if phase == 1 else (p2s, p2r)
        for half in range(2):
            for d in steps:
                arrive(piece(buf, half, phase, -d, *span(g, half)), ssem.at[g, half, d - 1], rsem.at[g, half, d - 1])

    def relay_start(buf, g):
        for half in range(2):
            r, n = span(g, half)
            for side, d in ((0, 1), (1, 3)):
                arrive(piece(buf, half, 2, -d, r, n), p2s.at[g, half, d - 1], p2r.at[g, half, d - 1])
                part = piece(buf, half, 2, -d, r + side * (n // 2), n // 2)
                send(part, part, rls.at[g, half, side], rlr.at[g, half, side], along(half, 2, d))

    def relay_wait(buf, g):
        for half in range(2):
            r, n = span(g, half)
            for side in range(2):
                arrive(piece(buf, half, 2, 2, r + side * (n // 2), n // 2), rls.at[g, half, side], rlr.at[g, half, side])

    load = pltpu.make_async_copy(bs_hbm, bs, bs_sem)
    load.start()
    wp[x, y, 0:32, :] = cq[...]
    wp[x, y, 32:64, :] = ck[...]
    wp[x, y, 64:96, :] = cv[...]
    wp[x, y, 96:224, 0:128] = co[0:128, :]
    wp[x, y, 96:224, 128:256] = co[128:256, :]
    wp[x, y, 224:352, :] = lq[...]
    wp[x, y, 352:480, :] = lk[...]
    wp[x, y, 480:608, :] = lv[...]
    wp[x, y, 608:736, 0:128] = lo[0:128, :]
    wp[x, y, 608:736, 128:256] = lo[128:256, :]

    barrier = pltpu.get_barrier_semaphore()
    beside = [wrap(c + 1, SIDE * SIDE), wrap(c - 1, SIDE * SIDE)]
    peers = [dev(wrap(x + d, SIDE), y, k, z) for d in (1, 2, 3)]
    peers += [dev(x, wrap(y + d, SIDE), k, z) for d in (1, 2, 3)]
    peers += [partner, up, down]
    peers += [(chip * 2 + core, z) for chip in beside for core in (0, 1)]
    for peer in peers:
        pl.semaphore_signal(barrier, inc=1, device_id=peer, device_id_type=MESH)
    pl.semaphore_wait(barrier, len(peers))

    phase_start(wp, 0, 1, (1, 2, 3))

    slot_row = bp_ref[...] - (seq * 128 - 64)
    load.wait()

    def slots(first, count):
        at = lax.broadcasted_iota(jnp.int32, (count, bp_ref.shape[1]), 0) + first
        return at == slot_row

    @pl.loop(0, 4)
    def _(i):
        first = pl.multiple_of(i * 64, 64)
        mask = slots(first, 64)
        ones = mask.astype(F32)
        count = jnp.maximum(jnp.sum(ones, axis=1, keepdims=True), 1.0)
        pooled[pl.ds(first, 64), :] = (dot(ones.astype(BF), bs[...]) / count).astype(BF)

    phase_wait(wp, 0, 1, (1, 2, 3))
    phase_start(wp, 0, 2, (1, 2, 3))
    for g in (1, 2, 3):
        phase_start(wp, g, 1, (1, 2, 3))
    phase_wait(wp, 0, 2, (1, 2, 3))
    cross_part = wp.at[:, :, pl.ds(0, 96), :]
    send(cross_part, wx, es.at[0], er.at[0], partner)
    for g in (1, 2, 3):
        phase_wait(wp, g, 1, (1, 2, 3))
        phase_start(wp, g, 2, (1, 3))
    own_at, other_at = k * 32, 32 - k * 32

    def fill(source, offset):
        @pl.loop(0, SIDE * SIDE)
        def _(chip):
            px, py = lax.div(chip, SIDE), lax.rem(chip, SIDE)
            at = pl.multiple_of(chip * 64 + offset, 32)
            for m in range(3):
                wf[m, pl.ds(at, 32), :] = source[px, py, m * 32 : (m + 1) * 32, :]

    fill(wp, own_at)
    arrive(wx, es.at[0], er.at[0])
    fill(wx, other_at)

    @pl.loop(0, 4)
    def _(i):
        part = pl.ds(pl.multiple_of(i * 256, 256), 256)
        kk[part, :] = dot(bs[part, :], wf[1]).astype(BF)
        vv[part, :] = dot(bs[part, :], wf[2]).astype(BF)

    @pl.loop(0, 4)
    def _(i):
        first = pl.multiple_of(i * 64, 64)
        part = pl.ds(first, 64)
        mask = slots(first, 64)
        query = dot(pooled[part, :], wf[0]).astype(BF)
        for h in range(2):
            cols = slice(h * 128, (h + 1) * 128)
            weight = jnp.where(mask, capped(dot_t(query[:, cols], kk[:, cols])), 0.0)
            total = jnp.sum(weight, axis=1, keepdims=True)
            total = jnp.where(total > 0.0, total, 1.0)
            wbuf[k, part, cols] = (dot(weight.astype(BF), vv[:, cols]) / total).astype(BF)

    send(wbuf.at[k], wbuf.at[k], es.at[1], er.at[1], partner)
    near = wrap(c + 2 * k - 1, SIDE * SIDE)
    edge = wbuf.at[k, pl.ds(pl.multiple_of(k * 192, 64), 64), :]
    for core in (0, 1):
        send(edge, e1b.at[1 - k], es.at[2 + core], er.at[3 - k], (near * 2 + core, z))
    relay_start(wp, 1)
    arrive(wbuf.at[1 - k], es.at[1], er.at[1])
    arrive(e1b.at[0], es.at[2], er.at[2])
    arrive(e1b.at[1], es.at[3], er.at[3])
    xbuf[0:64, :] = wbuf[0, 64:128, :] + e1b[0]
    xbuf[64:192, :] = wbuf[0, 128:256, :] + wbuf[1, 0:128, :]
    xbuf[192:256, :] = wbuf[1, 128:192, :] + e1b[1]
    relay_wait(wp, 1)

    def chunk_of(g, j):
        r, n = GROUPS[g]
        return wp[lax.div(j, SIDE), lax.rem(j, SIDE), r : r + n, :]

    def reduce_depth(w, part, hook):
        for u in range(UP):
            moves = [(u, wrap(z + UP - u, DEPTH), up)]
            if u < DOWN:
                moves.append((UP + u, wrap(z - DOWN + u, DEPTH), down))
            terms = [part(j) for _, j, _ in moves]
            for (slot, _, target), term in zip(moves, terms):
                if u:
                    arrive(rrecv.at[w, slot - 1], rss.at[w, slot - 1], rsr.at[w, slot - 1])
                    term = term + rrecv[w, slot - 1].astype(F32)
                rsend[w, slot] = term.astype(BF)
                send(rsend.at[w, slot], rrecv.at[w, slot], rss.at[w, slot], rsr.at[w, slot], target)
            hook(u)
        term = part(z)
        for slot in (DEPTH - 2, UP - 1):
            arrive(rrecv.at[w, slot], rss.at[w, slot], rsr.at[w, slot])
            term = term + rrecv[w, slot].astype(F32)
        return term

    def first_part(j):
        w = chunk_of(1, j)
        return dot(xbuf[:, 0:128], w[:, 0:128]) + dot(xbuf[:, 128:256], w[:, 128:256])

    def first_hook(u):
        if u == 4:
            relay_start(wp, 2)

    latent[...] = reduce_depth(0, first_part, first_hook).astype(BF)
    ag[z] = latent[...]

    def forward(u):
        moves = [(u, wrap(z - u, DEPTH), up)]
        if u < DOWN:
            moves.append((UP + u, wrap(z + u, DEPTH), down))
        for slot, j, target in moves:
            send(ag.at[j], ag.at[j], ags.at[slot], agr.at[slot], target)

    def project(js, fresh):
        pieces, weights = [], []
        squares = None
        for j in js:
            held = ag[j].astype(F32)
            squares = held * held if squares is None else squares + held * held
            pieces.append((held * gain[pl.ds(2 * j + k, 1), :]).astype(BF))
            weights.append(chunk_of(2, j))
        left = pieces[0] if len(js) == 1 else jnp.concatenate(pieces, axis=1)
        sq[...] = squares if fresh else sq[...] + squares
        for m in range(3):
            rows = [w[m * 128 : (m + 1) * 128, :] for w in weights]
            right = rows[0] if len(js) == 1 else jnp.concatenate(rows, axis=0)
            term = dot(left, right)
            for h in range(2):
                at = (h, slice(None), slice(m * 128, (m + 1) * 128))
                piece_of = term[:, h * 128 : (h + 1) * 128]
                acc[at] = piece_of if fresh else acc[at] + piece_of

    forward(0)
    relay_wait(wp, 2)
    project([z], True)
    relay_start(wp, 3)
    for u in range(UP):
        slots_now = [(u, wrap(z - 1 - u, DEPTH))]
        if u < DOWN:
            slots_now.append((UP + u, wrap(z + 1 + u, DEPTH)))
        for slot, j in slots_now:
            arrive(ag.at[j], ags.at[slot], agr.at[slot])
        if u + 1 < UP:
            forward(u + 1)
        project([j for _, j in slots_now], False)

    acc[1 - k, :, 384:512] = sq[...]
    send(acc.at[1 - k], e2, es.at[4], er.at[4], partner)
    arrive(e2, es.at[4], er.at[4])
    mean = jnp.sum(sq[...] + e2[:, 384:512], axis=1, keepdims=True) / (2 * DEPTH * 128)
    factor = lax.rsqrt(mean + EPS)

    def joined(m):
        cols = slice(m * 128, (m + 1) * 128)
        return ((acc[k, :, cols] + e2[:, cols]) * factor).astype(BF)

    kvb[x, y, :, 0:128] = joined(1)
    kvb[x, y, :, 128:256] = joined(2)
    phase_start(kvb, 4, 1, (1, 2, 3))
    qs[...] = joined(0)

    def attend(px, py, diagonal):
        keys, values = kvb[px, py, :, 0:128], kvb[px, py, :, 128:256]
        weight = capped(dot_t(qs[...], keys))
        if diagonal:
            shape = (ROWS, ROWS)
            seen = lax.broadcasted_iota(jnp.int32, shape, 1) <= lax.broadcasted_iota(jnp.int32, shape, 0)
            weight = jnp.where(seen, weight, 0.0)
        total = weight[:, 0:128] + weight[:, 128:256]
        value = dot(weight.astype(BF), values)
        oacc[...] = value if diagonal else oacc[...] + value
        lacc[...] = total if diagonal else lacc[...] + total

    attend(x, y, True)
    phase_wait(kvb, 4, 1, (1, 2, 3))
    phase_start(kvb, 4, 2, (1, 3))
    relay_start(kvb, 4)
    relay_wait(wp, 3)
    relay_wait(kvb, 4)

    @pl.loop(0, c)
    def _(chip):
        attend(lax.div(chip, SIDE), lax.rem(chip, SIDE), False)

    total = jnp.sum(lacc[...], axis=1, keepdims=True)
    att[k] = (oacc[...] / total).astype(BF)
    send(att.at[k], att.at[k], es.at[5], er.at[5], partner)
    arrive(att.at[1 - k], es.at[5], er.at[5])

    def second_part(j):
        w = chunk_of(3, j)
        return dot(att[0], w[:, 0:128]) + dot(att[1], w[:, 128:256])

    mixed = reduce_depth(1, second_part, lambda u: None)
    fin_s[...] = (latent[...].astype(F32) + mixed).astype(BF)
    theirs = fin_s.at[pl.ds(pl.multiple_of((1 - k) * 128, 128), 128), :]
    send(theirs, fin_r, es.at[6], er.at[6], partner)
    mine = pl.ds(pl.multiple_of(k * 128, 128), 128)
    out_ref[:, mine] = fin_s[mine, :]
    arrive(fin_r, es.at[6], er.at[6])
    out_ref[:, pl.ds(pl.multiple_of((1 - k) * 128, 128), 128)] = fin_r[...]
    for copy in started:
        copy.wait_send()


def per_device(
    byte_states, byte_patch, patch_len, cross_query, cross_key, cross_value, cross_out, norm_gain,
    latent_query, latent_key, latent_value, latent_out,
):
    vmem = pl.BlockSpec(memory_space=pltpu.VMEM)
    bytes_here, width = byte_states.shape
    dma = pltpu.SemaphoreType.DMA
    groups = len(GROUPS)
    block = (ROWS, HEAD_DIM)
    return pl.pallas_call(
        kernel,
        out_shape=jax.ShapeDtypeStruct((128, 256), BF),
        in_specs=[pl.BlockSpec(memory_space=pl.ANY)] + [vmem] * 10,
        out_specs=vmem,
        scratch_shapes=[
            pltpu.VMEM((bytes_here, width), BF),
            pltpu.VMEM((SIDE, SIDE, PACKED, 256), BF),
            pltpu.VMEM((SIDE, SIDE, 96, 256), BF),
            pltpu.VMEM((3, width, 256), BF),
            pltpu.VMEM((ROWS, width), BF),
            pltpu.VMEM((bytes_here, 256), BF),
            pltpu.VMEM((bytes_here, 256), BF),
            pltpu.VMEM((2, ROWS, 256), BF),
            pltpu.VMEM((2, 64, 256), BF),
            pltpu.VMEM((ROWS, 256), BF),
            pltpu.VMEM((2, DEPTH - 1) + block, BF),
            pltpu.VMEM((2, DEPTH - 1) + block, BF),
            pltpu.VMEM((DEPTH,) + block, BF),
            pltpu.VMEM((2, ROWS, 512), F32),
            pltpu.VMEM(block, F32),
            pltpu.VMEM((ROWS, 512), F32),
            pltpu.VMEM(block, BF),
            pltpu.VMEM((SIDE, SIDE, ROWS, 256), BF),
            pltpu.VMEM(block, F32),
            pltpu.VMEM(block, F32),
            pltpu.VMEM((2,) + block, BF),
            pltpu.VMEM(block, BF),
            pltpu.VMEM(block, BF),
            pltpu.VMEM((128, HEAD_DIM), BF),
            dma,
            dma((groups, 2, 3)),
            dma((groups, 2, 3)),
            dma((groups, 2, 3)),
            dma((groups, 2, 3)),
            dma((groups, 2, 2)),
            dma((groups, 2, 2)),
            dma((2, DEPTH - 1)),
            dma((2, DEPTH - 1)),
            dma((DEPTH - 1,)),
            dma((DEPTH - 1,)),
            dma((7,)),
            dma((7,)),
        ],
        compiler_params=pltpu.CompilerParams(
            collective_id=0, has_side_effects=True, vmem_limit_bytes=60 * 1024 * 1024
        ),
        name="patches",
    )(
        byte_states, byte_patch.reshape(1, -1), cross_query, cross_key, cross_value, cross_out,
        norm_gain.reshape(-1, HEAD_DIM), latent_query, latent_key, latent_value, latent_out,
    )


def solution(mesh):
    return jax.shard_map(
        per_device,
        mesh=mesh,
        in_specs=(
            P("seq", None), P("seq"), P(), P("seq", "tensor"), P("seq", "tensor"), P("seq", "tensor"),
            P("tensor", "seq"), P(), P("seq", "tensor"), P("seq", "tensor"), P("seq", "tensor"), P("tensor", "seq"),
        ),
        out_specs=P("seq", "tensor"),
        check_vma=False,
    )
```

time: 381 us -> 166 us (0.44)
  the two profiles are of different devices: /device:TPU:4 before, /device:TPU:1 now
where the time goes in v1:
time: 166 us; the launch traced here: 163 us
  Pallas kernels  162 us (98%)
    pallas_call x1, Pallas kernels, per_device(): pl.pallas_call(kernel, out_shape=jax.ShapeDtypeStruct((128, 256), BF), in...  162 us

profile of v1, /device:TPU:1, one launch (start us, length us, event | category | flops | bytes accessed | tf_op | source)
XLA Modules:
  0.0 163.0 jit_solution(16410964734951193416)
XLA Ops:
  0.0 161.5 %patches.1 = bf16[128,256]{1,0:T(8,128)(2,1)} custom-call(bf16[1024,1024]{1,0:T(8,128)(2,1)} %bs_hbm.1, s32[1,1024]{1,0:T(1,128)} %bitcast.3, bf16[32,256]{1,0:T(8,128)(2,1)} %cq.1, bf16[32,256]{1,0:T(8,128)(2,1)} %ck.1, bf16[32,256]{1,0:T(8,128)(2,1)} %cv.1, bf16[256,128]{1,0:T(8,128)(2,1)} %co.1, f32[32,128]{1,0:T(8,128)} %bitcast.2, bf16[128,256]{1,0:T(8,128)(2,1)} %lq.1, ...), custom_call_target="tpu_custom_call" | custom-call | tf_op jit(solution)/shard_map/patches/pallas_call | solution.py:354
  161.5 1.5 copy.13

commit v2 on v1

--- a/solution.py
+++ b/solution.py
@@ -18,11 +18,12 @@
 BF = jnp.bfloat16
 F32 = jnp.float32
 
-CROSS, OUT1, LATENT, OUT2 = (0, 96), (96, 128), (224, 384), (608, 128)
-GROUPS = (CROSS, OUT1, LATENT, OUT2, (0, ROWS))
-PACKED = 736
-UP = DEPTH // 2
-DOWN = DEPTH - 1 - UP
+GROUPS = ((0, 32), (0, 128), (128, 384), (512, 128), (0, ROWS))
+PACKED = 640
+HOPS = DEPTH // 4
+PARTS = 2
+STRIP = ROWS // PARTS
+PLACE = (slice(384, 512), slice(0, 128), slice(128, 256), slice(256, 384))
 
 
 def dot(a, b):
@@ -40,8 +41,8 @@
 def kernel(
     bs_hbm, bp_ref, cq, ck, cv, co, gain, lq, lk, lv, lo,
     out_ref,
-    bs, wp, wx, wf, pooled, kk, vv, wbuf, e1b, xbuf, rsend, rrecv, ag, acc, sq, e2, qs, kvb, oacc, lacc, att, latent, fin_s, fin_r,
-    bs_sem, p1s, p1r, p2s, p2r, rls, rlr, rss, rsr, ags, agr, es, er,
+    bs, wp, wc, pooled, onehot, wbuf, e1b, xbuf, rsend, rrecv, ag, acc, sq, e2, qs, kvb, oacc, lacc, att, latent, fin_s, fin_r,
+    bs_sem, p1s, p1r, p2s, p2r, rls, rlr, rss, rsr, ags, agr, es, er, kvs, kvr,
 ):
     seq, z = lax.axis_index("seq"), lax.axis_index("tensor")
     k, c = lax.rem(seq, 2), lax.div(seq, 2)
@@ -69,6 +70,7 @@
 
     partner = (seq + 1 - 2 * k, z)
     up, down = (seq, wrap(z + 1, DEPTH)), (seq, wrap(z - 1, DEPTH))
+    above, below = (seq, wrap(z + 2, DEPTH)), (seq, wrap(z - 2, DEPTH))
 
     def along(half, phase, d):
         if (half == 0) == (phase == 1):
@@ -77,6 +79,12 @@
 
     def piece(buf, half, phase, d, r, n):
         part = pl.ds(r, n)
+        if buf is wc:
+            if half == 0:
+                across = wrap(x + d, SIDE) if phase == 1 else slice(None)
+                return wc.at[across, y if phase == 1 else wrap(y + d, SIDE), k, :, part, :]
+            across = slice(None) if phase == 2 else wrap(y + d, SIDE)
+            return wc.at[x if phase == 1 else wrap(x + d, SIDE), across, k, :, part, :]
         if half == 0:
             return buf.at[wrap(x + d, SIDE), y, part, :] if phase == 1 else buf.at[:, wrap(y + d, SIDE), part, :]
         return buf.at[x, wrap(y + d, SIDE), part, :] if phase == 1 else buf.at[wrap(x + d, SIDE), :, part, :]
@@ -114,93 +122,96 @@
 
     load = pltpu.make_async_copy(bs_hbm, bs, bs_sem)
     load.start()
-    wp[x, y, 0:32, :] = cq[...]
-    wp[x, y, 32:64, :] = ck[...]
-    wp[x, y, 64:96, :] = cv[...]
-    wp[x, y, 96:224, 0:128] = co[0:128, :]
-    wp[x, y, 96:224, 128:256] = co[128:256, :]
-    wp[x, y, 224:352, :] = lq[...]
-    wp[x, y, 352:480, :] = lk[...]
-    wp[x, y, 480:608, :] = lv[...]
-    wp[x, y, 608:736, 0:128] = lo[0:128, :]
-    wp[x, y, 608:736, 128:256] = lo[128:256, :]
+    for m, shard in enumerate((cq, ck, cv)):
+        wc[x, y, k, m] = shard[...]
+    for r, shard in ((0, co), (512, lo)):
+        wp[x, y, r : r + 128, 0:128] = shard[0:128, :]
+        wp[x, y, r : r + 128, 128:256] = shard[128:256, :]
+    for m, shard in enumerate((lq, lk, lv)):
+        wp[x, y, 128 * (m + 1) : 128 * (m + 2), :] = shard[...]
 
     barrier = pltpu.get_barrier_semaphore()
     beside = [wrap(c + 1, SIDE * SIDE), wrap(c - 1, SIDE * SIDE)]
     peers = [dev(wrap(x + d, SIDE), y, k, z) for d in (1, 2, 3)]
     peers += [dev(x, wrap(y + d, SIDE), k, z) for d in (1, 2, 3)]
-    peers += [partner, up, down]
+    peers += [partner, up, down, above, below]
     peers += [(chip * 2 + core, z) for chip in beside for core in (0, 1)]
     for peer in peers:
         pl.semaphore_signal(barrier, inc=1, device_id=peer, device_id_type=MESH)
-    pl.semaphore_wait(barrier, len(peers))
-
-    phase_start(wp, 0, 1, (1, 2, 3))
-
     slot_row = bp_ref[...] - (seq * 128 - 64)
+
+    def slots(first, count):
+        shape = (ROWS, count)
+        return lax.broadcasted_iota(jnp.int32, shape, 0) == slot_row[:, first : first + count]
+
+    ones = slots(0, bs.shape[0]).astype(F32)
+    count = jnp.maximum(jnp.sum(ones, axis=1, keepdims=True), 1.0)
+    onehot[...] = ones.astype(BF)
     load.wait()
-
-    def slots(first, count):
-        at = lax.broadcasted_iota(jnp.int32, (count, bp_ref.shape[1]), 0) + first
-        return at == slot_row
 
     @pl.loop(0, 4)
     def _(i):
-        first = pl.multiple_of(i * 64, 64)
-        mask = slots(first, 64)
-        ones = mask.astype(F32)
-        count = jnp.maximum(jnp.sum(ones, axis=1, keepdims=True), 1.0)
-        pooled[pl.ds(first, 64), :] = (dot(ones.astype(BF), bs[...]) / count).astype(BF)
-
-    phase_wait(wp, 0, 1, (1, 2, 3))
-    phase_start(wp, 0, 2, (1, 2, 3))
-    for g in (1, 2, 3):
-        phase_start(wp, g, 1, (1, 2, 3))
-    phase_wait(wp, 0, 2, (1, 2, 3))
-    cross_part = wp.at[:, :, pl.ds(0, 96), :]
-    send(cross_part, wx, es.at[0], er.at[0], partner)
-    for g in (1, 2, 3):
-        phase_wait(wp, g, 1, (1, 2, 3))
-        phase_start(wp, g, 2, (1, 3))
-    own_at, other_at = k * 32, 32 - k * 32
-
-    def fill(source, offset):
-        @pl.loop(0, SIDE * SIDE)
-        def _(chip):
-            px, py = lax.div(chip, SIDE), lax.rem(chip, SIDE)
-            at = pl.multiple_of(chip * 64 + offset, 32)
-            for m in range(3):
-                wf[m, pl.ds(at, 32), :] = source[px, py, m * 32 : (m + 1) * 32, :]
-
-    fill(wp, own_at)
-    arrive(wx, es.at[0], er.at[0])
-    fill(wx, other_at)
-
-    @pl.loop(0, 4)
-    def _(i):
-        part = pl.ds(pl.multiple_of(i * 256, 256), 256)
-        kk[part, :] = dot(bs[part, :], wf[1]).astype(BF)
-        vv[part, :] = dot(bs[part, :], wf[2]).astype(BF)
-
-    @pl.loop(0, 4)
-    def _(i):
-        first = pl.multiple_of(i * 64, 64)
-        part = pl.ds(first, 64)
-        mask = slots(first, 64)
-        query = dot(pooled[part, :], wf[0]).astype(BF)
+        cols = pl.ds(pl.multiple_of(i * 256, 256), 256)
+        pooled[:, cols] = (dot(onehot[...], bs[:, cols]) / count).astype(BF)
+
+    pl.semaphore_wait(barrier, len(peers))
+
+    phase_start(wc, 0, 1, (1, 2, 3))
+    phase_start(wp, 1, 1, (1, 2, 3))
+
+    def hand_over(half, d):
+        held = piece(wc, half, 2, -d, *span(0, half))
+        send(held, held, es.at[7 + 4 * half + d], er.at[7 + 4 * half + d], partner)
+
+    phase_wait(wc, 0, 1, (1, 2, 3))
+    phase_start(wc, 0, 2, (1, 3, 2))
+    for half in range(2):
+        hand_over(half, 0)
+    phase_wait(wp, 1, 1, (1, 2, 3))
+    phase_start(wp, 1, 2, (1, 3))
+    for d in (1, 3, 2):
+        phase_wait(wc, 0, 2, (d,))
+        for half in range(2):
+            hand_over(half, d)
+    relay_start(wp, 1)
+    phase_start(wp, 2, 1, (1, 2, 3))
+    for half in range(2):
+        for d in range(SIDE):
+            rows = pl.ds(*span(0, half))
+            if half == 0:
+                theirs = wc.at[:, wrap(y - d, SIDE), 1 - k, :, rows, :]
+            else:
+                theirs = wc.at[wrap(x - d, SIDE), :, 1 - k, :, rows, :]
+            arrive(theirs, es.at[7 + 4 * half + d], er.at[7 + 4 * half + d])
+
+    def cross(m):
+        return wc[:, :, :, m].reshape(bs.shape[1], 256)
+
+    query = dot(pooled[...], cross(0)).astype(BF)
+    heads, totals = [0.0, 0.0], [0.0, 0.0]
+    for i in range(4):
+        part = slice(i * 256, (i + 1) * 256)
+        key = dot(bs[part, :], cross(1)).astype(BF)
+        value = dot(bs[part, :], cross(2)).astype(BF)
+        mask = slots(i * 256, 256)
         for h in range(2):
             cols = slice(h * 128, (h + 1) * 128)
-            weight = jnp.where(mask, capped(dot_t(query[:, cols], kk[:, cols])), 0.0)
-            total = jnp.sum(weight, axis=1, keepdims=True)
-            total = jnp.where(total > 0.0, total, 1.0)
-            wbuf[k, part, cols] = (dot(weight.astype(BF), vv[:, cols]) / total).astype(BF)
+            weight = jnp.where(mask, capped(dot_t(query[:, cols], key[:, cols])), 0.0)
+            totals[h] = totals[h] + weight[:, 0:128] + weight[:, 128:256]
+            heads[h] = heads[h] + dot(weight.astype(BF), value[:, cols])
+    for h in range(2):
+        total = jnp.sum(totals[h], axis=1, keepdims=True)
+        total = jnp.where(total > 0.0, total, 1.0)
+        wbuf[k, :, h * 128 : (h + 1) * 128] = (heads[h] / total).astype(BF)
 
     send(wbuf.at[k], wbuf.at[k], es.at[1], er.at[1], partner)
     near = wrap(c + 2 * k - 1, SIDE * SIDE)
     edge = wbuf.at[k, pl.ds(pl.multiple_of(k * 192, 64), 64), :]
     for core in (0, 1):
         send(edge, e1b.at[1 - k], es.at[2 + core], er.at[3 - k], (near * 2 + core, z))
-    relay_start(wp, 1)
+    phase_wait(wp, 2, 1, (1, 2, 3))
+    phase_start(wp, 2, 2, (1, 3))
+    phase_start(wp, 3, 1, (1, 2, 3))
     arrive(wbuf.at[1 - k], es.at[1], er.at[1])
     arrive(e1b.at[0], es.at[2], er.at[2])
     arrive(e1b.at[1], es.at[3], er.at[3])
@@ -213,42 +224,79 @@
         r, n = GROUPS[g]
         return wp[lax.div(j, SIDE), lax.rem(j, SIDE), r : r + n, :]
 
-    def reduce_depth(w, part, hook):
-        for u in range(UP):
-            moves = [(u, wrap(z + UP - u, DEPTH), up)]
-            if u < DOWN:
-                moves.append((UP + u, wrap(z - DOWN + u, DEPTH), down))
-            terms = [part(j) for _, j, _ in moves]
-            for (slot, _, target), term in zip(moves, terms):
-                if u:
-                    arrive(rrecv.at[w, slot - 1], rss.at[w, slot - 1], rsr.at[w, slot - 1])
-                    term = term + rrecv[w, slot - 1].astype(F32)
-                rsend[w, slot] = term.astype(BF)
-                send(rsend.at[w, slot], rrecv.at[w, slot], rss.at[w, slot], rsr.at[w, slot], target)
-            hook(u)
-        term = part(z)
-        for slot in (DEPTH - 2, UP - 1):
-            arrive(rrecv.at[w, slot], rss.at[w, slot], rsr.at[w, slot])
-            term = term + rrecv[w, slot].astype(F32)
-        return term
+    def main_slot(side, m):
+        return m if side == 0 else 2 * HOPS + m - 1
+
+    def side_slot(side, m):
+        return HOPS + m if side == 0 else 3 * HOPS - 1 + m
+
+    def received(w, slot, p):
+        rows = slice(p * STRIP, (p + 1) * STRIP)
+        arrive(rrecv.at[w, slot, rows], rss.at[w, slot, p], rsr.at[w, slot, p])
+        return rrecv[w, slot, rows].astype(F32)
+
+    def give(w, slot, p, value, target):
+        rows = slice(p * STRIP, (p + 1) * STRIP)
+        rsend[w, slot, rows] = value.astype(BF)
+        send(rsend.at[w, slot, rows], rrecv.at[w, slot, rows], rss.at[w, slot, p], rsr.at[w, slot, p], target)
+
+    def reduce_depth(w, part, hook, result):
+        def share(side, away):
+            return part(wrap(z + away if side == 0 else z - away, DEPTH))
+
+        def strips(term):
+            return [term[p * STRIP : (p + 1) * STRIP] for p in range(PARTS)]
+
+        far, near = (above, below), (up, down)
+        for p, strip in enumerate(strips(share(0, 2 * HOPS))):
+            give(w, main_slot(0, 0), p, strip, far[0])
+        for m in range(HOPS):
+            for side in range(2):
+                for p, strip in enumerate(strips(share(side, 2 * HOPS - 1 - 2 * m))):
+                    give(w, side_slot(side, m), p, strip, near[side])
+            away = 2 * (HOPS - 1 - m)
+            terms = [strips(share(side, away)) for side in range(2 if m + 1 < HOPS else 1)]
+            for p in range(PARTS):
+                sums = []
+                for side in range(2):
+                    held = received(w, side_slot(side, m), p)
+                    if side == 0 or m > 0:
+                        held = held + received(w, main_slot(side, m), p)
+                    sums.append(held)
+                if m + 1 < HOPS:
+                    for side in range(2):
+                        give(w, main_slot(side, m + 1), p, terms[side][p] + sums[side], far[side])
+                else:
+                    result(slice(p * STRIP, (p + 1) * STRIP), terms[0][p] + sums[0] + sums[1])
+            hook(m)
 
     def first_part(j):
         w = chunk_of(1, j)
         return dot(xbuf[:, 0:128], w[:, 0:128]) + dot(xbuf[:, 128:256], w[:, 128:256])
 
     def first_hook(u):
-        if u == 4:
+        if u == 0:
             relay_start(wp, 2)
-
-    latent[...] = reduce_depth(0, first_part, first_hook).astype(BF)
-    ag[z] = latent[...]
-
-    def forward(u):
-        moves = [(u, wrap(z - u, DEPTH), up)]
-        if u < DOWN:
-            moves.append((UP + u, wrap(z + u, DEPTH), down))
-        for slot, j, target in moves:
-            send(ag.at[j], ag.at[j], ags.at[slot], agr.at[slot], target)
+        if u == 1:
+            phase_wait(wp, 3, 1, (1, 2, 3))
+            phase_start(wp, 3, 2, (1, 3))
+
+    def pass_on(m, p):
+        part = pl.ds(p * STRIP, STRIP)
+        for side, far, near in ((0, above, up), (1, below, down)):
+            strip = ag.at[wrap(z - 2 * m if side == 0 else z + 2 * m, DEPTH), part]
+            if side == 0 or m + 1 < HOPS:
+                slot = main_slot(side, m + side)
+                send(strip, strip, ags.at[slot, p], agr.at[slot, p], far)
+            slot = side_slot(side, m)
+            send(strip, strip, ags.at[slot, p], agr.at[slot, p], near)
+
+    def first_result(rows, value):
+        ag[z, rows] = value.astype(BF)
+        latent[rows] = ag[z, rows]
+        pass_on(0, rows.start // STRIP)
+
+    reduce_depth(0, first_part, first_hook, first_result)
 
     def project(js, fresh):
         pieces, weights = [], []
@@ -265,37 +313,79 @@
             right = rows[0] if len(js) == 1 else jnp.concatenate(rows, axis=0)
             term = dot(left, right)
             for h in range(2):
-                at = (h, slice(None), slice(m * 128, (m + 1) * 128))
+                at = (h, slice(None), PLACE[m])
                 piece_of = term[:, h * 128 : (h + 1) * 128]
                 acc[at] = piece_of if fresh else acc[at] + piece_of
 
-    forward(0)
     relay_wait(wp, 2)
     project([z], True)
     relay_start(wp, 3)
-    for u in range(UP):
-        slots_now = [(u, wrap(z - 1 - u, DEPTH))]
-        if u < DOWN:
-            slots_now.append((UP + u, wrap(z + 1 + u, DEPTH)))
-        for slot, j in slots_now:
-            arrive(ag.at[j], ags.at[slot], agr.at[slot])
-        if u + 1 < UP:
-            forward(u + 1)
-        project([j for _, j in slots_now], False)
-
-    acc[1 - k, :, 384:512] = sq[...]
-    send(acc.at[1 - k], e2, es.at[4], er.at[4], partner)
-    arrive(e2, es.at[4], er.at[4])
-    mean = jnp.sum(sq[...] + e2[:, 384:512], axis=1, keepdims=True) / (2 * DEPTH * 128)
+    def take(j, slot, p):
+        arrive(ag.at[j, pl.ds(p * STRIP, STRIP)], ags.at[slot, p], agr.at[slot, p])
+
+    for m in range(HOPS):
+        mains = [(main_slot(0, m), wrap(z - 2 * (m + 1), DEPTH))]
+        if m + 1 < HOPS:
+            mains.append((main_slot(1, m + 1), wrap(z + 2 * (m + 1), DEPTH)))
+        sides = [(side_slot(0, m), wrap(z - 1 - 2 * m, DEPTH)), (side_slot(1, m), wrap(z + 1 + 2 * m, DEPTH))]
+        if m + 1 == HOPS:
+            mains, sides = sides, mains
+        for p in range(PARTS):
+            for slot, j in mains:
+                take(j, slot, p)
+            if m + 1 < HOPS:
+                pass_on(m + 1, p)
+        if m + 1 == HOPS:
+            project([j for _, j in mains], False)
+        for slot, j in sides:
+            for p in range(PARTS):
+                take(j, slot, p)
+        project([j for _, j in sides], False)
+        if m + 1 < HOPS:
+            project([j for _, j in mains], False)
+
+    acc[1 - k, :, PLACE[3]] = sq[...]
+    first, last = (slice(None), pl.ds(0, 384)), (slice(None), pl.ds(384, 128))
+    send(acc.at[(1 - k,) + first], e2.at[first], es.at[4], er.at[4], partner)
+    send(acc.at[(1 - k,) + last], e2.at[last], es.at[0], er.at[0], partner)
+    arrive(e2.at[first], es.at[4], er.at[4])
+    mean = jnp.sum(sq[...] + e2[:, PLACE[3]], axis=1, keepdims=True) / (2 * DEPTH * 128)
     factor = lax.rsqrt(mean + EPS)
 
     def joined(m):
-        cols = slice(m * 128, (m + 1) * 128)
-        return ((acc[k, :, cols] + e2[:, cols]) * factor).astype(BF)
+        return ((acc[k, :, PLACE[m]] + e2[:, PLACE[m]]) * factor).astype(BF)
 
     kvb[x, y, :, 0:128] = joined(1)
     kvb[x, y, :, 128:256] = joined(2)
-    phase_start(kvb, 4, 1, (1, 2, 3))
+
+    def kv_piece(half, q, d, r, n):
+        px, py = (wrap(x - q, SIDE), wrap(y - d, SIDE)) if half == 0 else (wrap(x - d, SIDE), wrap(y - q, SIDE))
+        return kvb.at[px, py, pl.ds(r, n), :]
+
+    def kv_on(q):
+        for half in range(2):
+            held = kv_piece(half, q, 0, *span(4, half))
+            for side, d in ((0, 1), (1, 3)):
+                send(held, held, kvs.at[half, side, q], kvr.at[half, side, q], along(half, 2, d))
+
+    def kv_relay(q):
+        for half in range(2):
+            r, n = span(4, half)
+            for side, d in ((0, 1), (1, 3)):
+                arrive(kv_piece(half, q, d, r, n), kvs.at[half, side, q], kvr.at[half, side, q])
+                part = kv_piece(half, q, d, r + side * (n // 2), n // 2)
+                send(part, part, kvs.at[half, 2 + side, q], kvr.at[half, 2 + side, q], along(half, 2, d))
+
+    def kv_last(q):
+        for half in range(2):
+            r, n = span(4, half)
+            for side in range(2):
+                part = kv_piece(half, q, 2, r + side * (n // 2), n // 2)
+                arrive(part, kvs.at[half, 2 + side, q], kvr.at[half, 2 + side, q])
+
+    phase_start(kvb, 4, 1, (1, 3, 2))
+    kv_on(0)
+    arrive(e2.at[last], es.at[0], er.at[0])
     qs[...] = joined(0)
 
     def attend(px, py, diagonal):
@@ -311,11 +401,17 @@
         lacc[...] = total if diagonal else lacc[...] + total
 
     attend(x, y, True)
-    phase_wait(kvb, 4, 1, (1, 2, 3))
-    phase_start(kvb, 4, 2, (1, 3))
-    relay_start(kvb, 4)
+    for d in (1, 3):
+        phase_wait(kvb, 4, 1, (d,))
+        kv_on(d)
+    kv_relay(0)
+    phase_wait(kvb, 4, 1, (2,))
+    kv_on(2)
+    for q in (1, 3, 2):
+        kv_relay(q)
     relay_wait(wp, 3)
-    relay_wait(kvb, 4)
+    for q in range(SIDE):
+        kv_last(q)
 
     @pl.loop(0, c)
     def _(chip):
@@ -330,8 +426,10 @@
         w = chunk_of(3, j)
         return dot(att[0], w[:, 0:128]) + dot(att[1], w[:, 128:256])
 
-    mixed = reduce_depth(1, second_part, lambda u: None)
-    fin_s[...] = (latent[...].astype(F32) + mixed).astype(BF)
+    def second_result(rows, value):
+        fin_s[rows] = (latent[rows].astype(F32) + value).astype(BF)
+
+    reduce_depth(1, second_part, lambda m: None, second_result)
     theirs = fin_s.at[pl.ds(pl.multiple_of((1 - k) * 128, 128), 128), :]
     send(theirs, fin_r, es.at[6], er.at[6], partner)
     mine = pl.ds(pl.multiple_of(k * 128, 128), 128)
@@ -359,11 +457,9 @@
         scratch_shapes=[
             pltpu.VMEM((bytes_here, width), BF),
             pltpu.VMEM((SIDE, SIDE, PACKED, 256), BF),
-            pltpu.VMEM((SIDE, SIDE, 96, 256), BF),
-            pltpu.VMEM((3, width, 256), BF),
+            pltpu.VMEM((SIDE, SIDE, 2, 3, 32, 256), BF),
             pltpu.VMEM((ROWS, width), BF),
-            pltpu.VMEM((bytes_here, 256), BF),
-            pltpu.VMEM((bytes_here, 256), BF),
+            pltpu.VMEM((ROWS, bytes_here), BF),
             pltpu.VMEM((2, ROWS, 256), BF),
             pltpu.VMEM((2, 64, 256), BF),
             pltpu.VMEM((ROWS, 256), BF),
@@ -388,12 +484,14 @@
             dma((groups, 2, 3)),
             dma((groups, 2, 2)),
             dma((groups, 2, 2)),
-            dma((2, DEPTH - 1)),
-            dma((2, DEPTH - 1)),
-            dma((DEPTH - 1,)),
-            dma((DEPTH - 1,)),
-            dma((7,)),
-            dma((7,)),
+            dma((2, DEPTH - 1, PARTS)),
+            dma((2, DEPTH - 1, PARTS)),
+            dma((DEPTH - 1, PARTS)),
+            dma((DEPTH - 1, PARTS)),
+            dma((15,)),
+            dma((15,)),
+            dma((2, SIDE, SIDE)),
+            dma((2, SIDE, SIDE)),
         ],
         compiler_params=pltpu.CompilerParams(
             collective_id=0, has_side_effects=True, vmem_limit_bytes=60 * 1024 * 1024

time: 166 us -> 135 us (0.81)
  the two profiles are of different devices: /device:TPU:1 before, /device:TPU:7 now
where the time goes in v2:
time: 135 us
  Pallas kernels  134 us (99%)
  local copies, waits for them, and re-layouts  1.47 us (1%)
    pallas_call x1, Pallas kernels, per_device(): pl.pallas_call(kernel, out_shape=jax.ShapeDtypeStruct((128, 256), BF), in...  134 us

profile of v2, /device:TPU:7, one launch (start us, length us, event | category | flops | bytes accessed | tf_op | source)
XLA Modules:
  0.0 135.1 jit_solution(12794656424706152261)
XLA Ops:
  0.0 133.6 %patches.1 = bf16[128,256]{1,0:T(8,128)(2,1)} custom-call(bf16[1024,1024]{1,0:T(8,128)(2,1)} %bs_hbm.1, s32[1,1024]{1,0:T(1,128)} %bitcast.3, bf16[32,256]{1,0:T(8,128)(2,1)} %cq.1, bf16[32,256]{1,0:T(8,128)(2,1)} %ck.1, bf16[32,256]{1,0:T(8,128)(2,1)} %cv.1, bf16[256,128]{1,0:T(8,128)(2,1)} %co.1, f32[32,128]{1,0:T(8,128)} %bitcast.2, bf16[128,256]{1,0:T(8,128)(2,1)} %lq.1, ...), custom_call_target="tpu_custom_call" | custom-call | tf_op jit(solution)/shard_map/patches/pallas_call | solution.py:452
  133.6 1.5 %copy.13 = bf16[128,256]{1,0:T(8,128)(2,1)} copy(bf16[128,256]{1,0:T(8,128)(2,1)} %patches.1) | data formatting | bytes 131072

commit v3 on v2

--- a/solution.py
+++ b/solution.py
@@ -174,7 +174,6 @@
         for half in range(2):
             hand_over(half, d)
     relay_start(wp, 1)
-    phase_start(wp, 2, 1, (1, 2, 3))
     for half in range(2):
         for d in range(SIDE):
             rows = pl.ds(*span(0, half))
@@ -209,9 +208,7 @@
     edge = wbuf.at[k, pl.ds(pl.multiple_of(k * 192, 64), 64), :]
     for core in (0, 1):
         send(edge, e1b.at[1 - k], es.at[2 + core], er.at[3 - k], (near * 2 + core, z))
-    phase_wait(wp, 2, 1, (1, 2, 3))
-    phase_start(wp, 2, 2, (1, 3))
-    phase_start(wp, 3, 1, (1, 2, 3))
+    phase_start(wp, 2, 1, (1, 3, 2))
     arrive(wbuf.at[1 - k], es.at[1], er.at[1])
     arrive(e1b.at[0], es.at[2], er.at[2])
     arrive(e1b.at[1], es.at[3], er.at[3])
@@ -248,26 +245,31 @@
             return [term[p * STRIP : (p + 1) * STRIP] for p in range(PARTS)]
 
         far, near = (above, below), (up, down)
-        for p, strip in enumerate(strips(share(0, 2 * HOPS))):
-            give(w, main_slot(0, 0), p, strip, far[0])
+
+        def give_step(m, p, mains, sides):
+            for side, main in mains.items():
+                give(w, main_slot(side, m), p, main, far[side])
+            for side in range(2):
+                give(w, side_slot(side, m), p, sides[side][p], near[side])
+
+        first_main = strips(share(0, 2 * HOPS))
+        first_sides = [strips(share(side, 2 * HOPS - 1)) for side in range(2)]
+        give_step(0, 0, {0: first_main[0]}, first_sides)
+        early = [received(w, side_slot(side, 0), 0) for side in range(2)]
+        give_step(0, 1, {0: first_main[1]}, first_sides)
         for m in range(HOPS):
-            for side in range(2):
-                for p, strip in enumerate(strips(share(side, 2 * HOPS - 1 - 2 * m))):
-                    give(w, side_slot(side, m), p, strip, near[side])
+            last = m + 1 == HOPS
             away = 2 * (HOPS - 1 - m)
-            terms = [strips(share(side, away)) for side in range(2 if m + 1 < HOPS else 1)]
+            terms = [strips(share(side, away)) for side in range(1 if last else 2)]
+            sides = None if last else [strips(share(side, away - 1)) for side in range(2)]
             for p in range(PARTS):
-                sums = []
-                for side in range(2):
-                    held = received(w, side_slot(side, m), p)
-                    if side == 0 or m > 0:
-                        held = held + received(w, main_slot(side, m), p)
-                    sums.append(held)
-                if m + 1 < HOPS:
-                    for side in range(2):
-                        give(w, main_slot(side, m + 1), p, terms[side][p] + sums[side], far[side])
+                sums = early if (m, p) == (0, 0) else [received(w, side_slot(side, m), p) for side in range(2)]
+                for side in range(2 if m else 1):
+                    sums[side] = sums[side] + received(w, main_slot(side, m), p)
+                if last:
+                    result(slice(p * STRIP, (p + 1) * STRIP), terms[0][p] + sums[0] + sums[1])
                 else:
-                    result(slice(p * STRIP, (p + 1) * STRIP), terms[0][p] + sums[0] + sums[1])
+                    give_step(m + 1, p, {side: terms[side][p] + sums[side] for side in range(2)}, sides)
             hook(m)
 
     def first_part(j):
@@ -276,10 +278,12 @@
 
     def first_hook(u):
         if u == 0:
+            phase_wait(wp, 2, 1, (1, 2, 3))
+            phase_start(wp, 2, 2, (1, 3))
+        if u == 2:
             relay_start(wp, 2)
-        if u == 1:
-            phase_wait(wp, 3, 1, (1, 2, 3))
-            phase_start(wp, 3, 2, (1, 3))
+        if u == 3:
+            phase_start(wp, 3, 1, (1, 2, 3))
 
     def pass_on(m, p):
         part = pl.ds(p * STRIP, STRIP)
@@ -319,30 +323,37 @@
 
     relay_wait(wp, 2)
     project([z], True)
-    relay_start(wp, 3)
     def take(j, slot, p):
         arrive(ag.at[j, pl.ds(p * STRIP, STRIP)], ags.at[slot, p], agr.at[slot, p])
 
+    held = None
     for m in range(HOPS):
         mains = [(main_slot(0, m), wrap(z - 2 * (m + 1), DEPTH))]
         if m + 1 < HOPS:
             mains.append((main_slot(1, m + 1), wrap(z + 2 * (m + 1), DEPTH)))
         sides = [(side_slot(0, m), wrap(z - 1 - 2 * m, DEPTH)), (side_slot(1, m), wrap(z + 1 + 2 * m, DEPTH))]
-        if m + 1 == HOPS:
-            mains, sides = sides, mains
         for p in range(PARTS):
+            if m + 1 == HOPS and p == 1:
+                for slot, j in sides:
+                    for strip in range(PARTS):
+                        take(j, slot, strip)
+                project([j for _, j in sides], False)
             for slot, j in mains:
                 take(j, slot, p)
             if m + 1 < HOPS:
                 pass_on(m + 1, p)
-        if m + 1 == HOPS:
-            project([j for _, j in mains], False)
-        for slot, j in sides:
-            for p in range(PARTS):
-                take(j, slot, p)
-        project([j for _, j in sides], False)
+            if p == 0 and held is not None:
+                project(held, False)
         if m + 1 < HOPS:
-            project([j for _, j in mains], False)
+            for slot, j in sides:
+                for p in range(PARTS):
+                    take(j, slot, p)
+            project([j for _, j in sides], False)
+        held = [j for _, j in mains]
+        if m == 1:
+            phase_wait(wp, 3, 1, (1, 2, 3))
+            phase_start(wp, 3, 2, (1, 3))
+    project(held, False)
 
     acc[1 - k, :, PLACE[3]] = sq[...]
     first, last = (slice(None), pl.ds(0, 384)), (slice(None), pl.ds(384, 128))
@@ -388,34 +399,42 @@
     arrive(e2.at[last], es.at[0], er.at[0])
     qs[...] = joined(0)
 
-    def attend(px, py, diagonal):
-        keys, values = kvb[px, py, :, 0:128], kvb[px, py, :, 128:256]
-        weight = capped(dot_t(qs[...], keys))
-        if diagonal:
-            shape = (ROWS, ROWS)
-            seen = lax.broadcasted_iota(jnp.int32, shape, 1) <= lax.broadcasted_iota(jnp.int32, shape, 0)
-            weight = jnp.where(seen, weight, 0.0)
-        total = weight[:, 0:128] + weight[:, 128:256]
-        value = dot(weight.astype(BF), values)
-        oacc[...] = value if diagonal else oacc[...] + value
-        lacc[...] = total if diagonal else lacc[...] + total
-
-    attend(x, y, True)
+    def attend(blocks):
+        value = total = None
+        for dx, dy in blocks:
+            px, py = wrap(x + dx, SIDE), wrap(y + dy, SIDE)
+            weight = capped(dot_t(qs[...], kvb[px, py, :, 0:128]))
+            if (dx, dy) == (0, 0):
+                shape = (ROWS, ROWS)
+                seen = lax.broadcasted_iota(jnp.int32, shape, 1) <= lax.broadcasted_iota(jnp.int32, shape, 0)
+                weight = jnp.where(seen, weight, 0.0)
+            else:
+                weight = weight * jnp.where(px * SIDE + py < c, 1.0, 0.0)
+            term = dot(weight.astype(BF), kvb[px, py, :, 128:256])
+            mass = weight[:, 0:128] + weight[:, 128:256]
+            value = term if value is None else value + term
+            total = mass if total is None else total + mass
+        own = blocks[0] == (0, 0)
+        oacc[...] = value if own else oacc[...] + value
+        lacc[...] = total if own else lacc[...] + total
+
+    attend([(0, 0)])
     for d in (1, 3):
         phase_wait(kvb, 4, 1, (d,))
         kv_on(d)
     kv_relay(0)
     phase_wait(kvb, 4, 1, (2,))
     kv_on(2)
-    for q in (1, 3, 2):
-        kv_relay(q)
-    relay_wait(wp, 3)
+    attend([(1, 0), (3, 0), (0, 1), (0, 3)])
+    kv_relay(1)
+    kv_relay(3)
+    attend([(1, 1), (1, 3), (3, 1), (3, 3)])
+    kv_relay(2)
+    relay_start(wp, 3)
     for q in range(SIDE):
         kv_last(q)
-
-    @pl.loop(0, c)
-    def _(chip):
-        attend(lax.div(chip, SIDE), lax.rem(chip, SIDE), False)
+    attend([(2, 0), (2, 1), (2, 2), (2, 3), (0, 2), (1, 2), (3, 2)])
+    relay_wait(wp, 3)
 
     total = jnp.sum(lacc[...], axis=1, keepdims=True)
     att[k] = (oacc[...] / total).astype(BF)

time: 135 us -> 128 us (0.948)
  the two profiles are of different devices: /device:TPU:7 before, /device:TPU:1 now
where the time goes in v3:
time: 128 us; the launch traced here: 127 us
  Pallas kernels  126 us (98%)
  local copies, waits for them, and re-layouts  1.47 us (1%)
    pallas_call x1, Pallas kernels, per_device(): pl.pallas_call(kernel, out_shape=jax.ShapeDtypeStruct((128, 256), BF), in...  126 us

profile of v3, /device:TPU:1, one launch (start us, length us, event | category | flops | bytes accessed | tf_op | source)
XLA Modules:
  0.0 127.3 jit_solution(7566237275400310263)
XLA Ops:
  0.0 125.9 %patches.1 = bf16[128,256]{1,0:T(8,128)(2,1)} custom-call(bf16[1024,1024]{1,0:T(8,128)(2,1)} %bs_hbm.1, s32[1,1024]{1,0:T(1,128)} %bitcast.3, bf16[32,256]{1,0:T(8,128)(2,1)} %cq.1, bf16[32,256]{1,0:T(8,128)(2,1)} %ck.1, bf16[32,256]{1,0:T(8,128)(2,1)} %cv.1, bf16[256,128]{1,0:T(8,128)(2,1)} %co.1, f32[32,128]{1,0:T(8,128)} %bitcast.2, bf16[128,256]{1,0:T(8,128)(2,1)} %lq.1, ...), custom_call_target="tpu_custom_call" | custom-call | tf_op jit(solution)/shard_map/patches/pallas_call | solution.py:471
  125.9 1.5 %copy.13 = bf16[128,256]{1,0:T(8,128)(2,1)} copy(bf16[128,256]{1,0:T(8,128)(2,1)} %patches.1) | data formatting | bytes 131072

commit v4 on v3

--- a/solution.py
+++ b/solution.py
@@ -21,7 +21,7 @@
 GROUPS = ((0, 32), (0, 128), (128, 384), (512, 128), (0, ROWS))
 PACKED = 640
 HOPS = DEPTH // 4
-PARTS = 2
+PARTS = 4
 STRIP = ROWS // PARTS
 PLACE = (slice(384, 512), slice(0, 128), slice(128, 256), slice(256, 384))
 
@@ -186,6 +186,7 @@
     def cross(m):
         return wc[:, :, :, m].reshape(bs.shape[1], 256)
 
+    phase_start(wp, 2, 1, (1, 3, 2))
     query = dot(pooled[...], cross(0)).astype(BF)
     heads, totals = [0.0, 0.0], [0.0, 0.0]
     for i in range(4):
@@ -208,7 +209,6 @@
     edge = wbuf.at[k, pl.ds(pl.multiple_of(k * 192, 64), 64), :]
     for core in (0, 1):
         send(edge, e1b.at[1 - k], es.at[2 + core], er.at[3 - k], (near * 2 + core, z))
-    phase_start(wp, 2, 1, (1, 3, 2))
     arrive(wbuf.at[1 - k], es.at[1], er.at[1])
     arrive(e1b.at[0], es.at[2], er.at[2])
     arrive(e1b.at[1], es.at[3], er.at[3])
@@ -216,6 +216,8 @@
     xbuf[64:192, :] = wbuf[0, 128:256, :] + wbuf[1, 0:128, :]
     xbuf[192:256, :] = wbuf[1, 128:192, :] + e1b[1]
     relay_wait(wp, 1)
+    phase_wait(wp, 2, 1, (1, 2, 3))
+    phase_start(wp, 2, 2, (1, 3))
 
     def chunk_of(g, j):
         r, n = GROUPS[g]
@@ -254,16 +256,15 @@
 
         first_main = strips(share(0, 2 * HOPS))
         first_sides = [strips(share(side, 2 * HOPS - 1)) for side in range(2)]
-        give_step(0, 0, {0: first_main[0]}, first_sides)
-        early = [received(w, side_slot(side, 0), 0) for side in range(2)]
-        give_step(0, 1, {0: first_main[1]}, first_sides)
+        for p in range(PARTS):
+            give_step(0, p, {0: first_main[p]}, first_sides)
         for m in range(HOPS):
             last = m + 1 == HOPS
             away = 2 * (HOPS - 1 - m)
             terms = [strips(share(side, away)) for side in range(1 if last else 2)]
             sides = None if last else [strips(share(side, away - 1)) for side in range(2)]
             for p in range(PARTS):
-                sums = early if (m, p) == (0, 0) else [received(w, side_slot(side, m), p) for side in range(2)]
+                sums = [received(w, side_slot(side, m), p) for side in range(2)]
                 for side in range(2 if m else 1):
                     sums[side] = sums[side] + received(w, main_slot(side, m), p)
                 if last:
@@ -277,12 +278,9 @@
         return dot(xbuf[:, 0:128], w[:, 0:128]) + dot(xbuf[:, 128:256], w[:, 128:256])
 
     def first_hook(u):
-        if u == 0:
-            phase_wait(wp, 2, 1, (1, 2, 3))
-            phase_start(wp, 2, 2, (1, 3))
+        if u == 1:
+            relay_start(wp, 2)
         if u == 2:
-            relay_start(wp, 2)
-        if u == 3:
             phase_start(wp, 3, 1, (1, 2, 3))
 
     def pass_on(m, p):
@@ -333,7 +331,7 @@
             mains.append((main_slot(1, m + 1), wrap(z + 2 * (m + 1), DEPTH)))
         sides = [(side_slot(0, m), wrap(z - 1 - 2 * m, DEPTH)), (side_slot(1, m), wrap(z + 1 + 2 * m, DEPTH))]
         for p in range(PARTS):
-            if m + 1 == HOPS and p == 1:
+            if m + 1 == HOPS and p == PARTS - 1:
                 for slot, j in sides:
                     for strip in range(PARTS):
                         take(j, slot, strip)
@@ -431,9 +429,13 @@
     attend([(1, 1), (1, 3), (3, 1), (3, 3)])
     kv_relay(2)
     relay_start(wp, 3)
-    for q in range(SIDE):
-        kv_last(q)
-    attend([(2, 0), (2, 1), (2, 2), (2, 3), (0, 2), (1, 2), (3, 2)])
+    kv_last(0)
+    attend([(2, 0), (0, 2)])
+    kv_last(1)
+    kv_last(3)
+    attend([(2, 1), (2, 3), (1, 2), (3, 2)])
+    kv_last(2)
+    attend([(2, 2)])
     relay_wait(wp, 3)
 
     total = jnp.sum(lacc[...], axis=1, keepdims=True)

time: 128 us -> 122 us (0.953)
  Pallas kernels: 126 us -> 121 us
    pallas_call x1, Pallas kernels: 126 us -> 121 us  [per_device(): pl.pallas_call(kernel, out_shape=jax.ShapeDtypeStruct((128, 256), BF), in...]
where the time goes in v4:
time: 122 us
  Pallas kernels  121 us (99%)
  local copies, waits for them, and re-layouts  1.47 us (1%)
    pallas_call x1, Pallas kernels, per_device(): pl.pallas_call(kernel, out_shape=jax.ShapeDtypeStruct((128, 256), BF), in...  121 us

profile of v4, /device:TPU:1, one launch (start us, length us, event | category | flops | bytes accessed | tf_op | source)
XLA Modules:
  0.0 122.2 jit_solution(1925036189716321)
XLA Ops:
  0.0 120.7 %patches.1 = bf16[128,256]{1,0:T(8,128)(2,1)} custom-call(bf16[1024,1024]{1,0:T(8,128)(2,1)} %bs_hbm.1, s32[1,1024]{1,0:T(1,128)} %bitcast.3, bf16[32,256]{1,0:T(8,128)(2,1)} %cq.1, bf16[32,256]{1,0:T(8,128)(2,1)} %ck.1, bf16[32,256]{1,0:T(8,128)(2,1)} %cv.1, bf16[256,128]{1,0:T(8,128)(2,1)} %co.1, f32[32,128]{1,0:T(8,128)} %bitcast.2, bf16[128,256]{1,0:T(8,128)(2,1)} %lq.1, ...), custom_call_target="tpu_custom_call" | custom-call | tf_op jit(solution)/shard_map/patches/pallas_call | solution.py:473
  120.7 1.5 %copy.13 = bf16[128,256]{1,0:T(8,128)(2,1)} copy(bf16[128,256]{1,0:T(8,128)(2,1)} %patches.1) | data formatting | bytes 131072

commit v5 on v4

--- a/solution.py
+++ b/solution.py
@@ -23,6 +23,7 @@
 HOPS = DEPTH // 4
 PARTS = 4
 STRIP = ROWS // PARTS
+ORDER = (1, 2, 0, 3)
 PLACE = (slice(384, 512), slice(0, 128), slice(128, 256), slice(256, 384))
 
 
@@ -39,9 +40,9 @@
 
 
 def kernel(
-    bs_hbm, bp_ref, cq, ck, cv, co, gain, lq, lk, lv, lo,
+    bs_in, bp_in, cq, ck, cv, co, gain_in, lq, lk, lv, lo,
     out_ref,
-    bs, wp, wc, pooled, onehot, wbuf, e1b, xbuf, rsend, rrecv, ag, acc, sq, e2, qs, kvb, oacc, lacc, att, latent, fin_s, fin_r,
+    bs, bp_ref, gain, wp, wc, pooled, onehot, wbuf, e1b, xbuf, rsend, rrecv, ag, acc, sq, e2, qs, kvb, oacc, lacc, att, latent, fin_s, fin_r,
     bs_sem, p1s, p1r, p2s, p2r, rls, rlr, rss, rsr, ags, agr, es, er, kvs, kvr,
 ):
     seq, z = lax.axis_index("seq"), lax.axis_index("tensor")
@@ -120,15 +121,15 @@
             for side in range(2):
                 arrive(piece(buf, half, 2, 2, r + side * (n // 2), n // 2), rls.at[g, half, side], rlr.at[g, half, side])
 
-    load = pltpu.make_async_copy(bs_hbm, bs, bs_sem)
-    load.start()
-    for m, shard in enumerate((cq, ck, cv)):
-        wc[x, y, k, m] = shard[...]
+    low, high = pl.ds(0, 128), pl.ds(128, 128)
+    moves = [(bp_in, bp_ref), (bs_in, bs), (gain_in, gain)]
+    moves += [(shard, wc.at[x, y, k, m]) for m, shard in enumerate((cq, ck, cv))]
     for r, shard in ((0, co), (512, lo)):
-        wp[x, y, r : r + 128, 0:128] = shard[0:128, :]
-        wp[x, y, r : r + 128, 128:256] = shard[128:256, :]
-    for m, shard in enumerate((lq, lk, lv)):
-        wp[x, y, 128 * (m + 1) : 128 * (m + 2), :] = shard[...]
+        moves += [(shard.at[half, :], wp.at[x, y, pl.ds(r, 128), half]) for half in (low, high)]
+    moves += [(shard, wp.at[x, y, pl.ds(128 * (m + 1), 128), :]) for m, shard in enumerate((lq, lk, lv))]
+    loads = [pltpu.make_async_copy(src, dst, bs_sem.at[n]) for n, (src, dst) in enumerate(moves)]
+    for copy in loads:
+        copy.start()
 
     barrier = pltpu.get_barrier_semaphore()
     beside = [wrap(c + 1, SIDE * SIDE), wrap(c - 1, SIDE * SIDE)]
@@ -138,6 +139,7 @@
     peers += [(chip * 2 + core, z) for chip in beside for core in (0, 1)]
     for peer in peers:
         pl.semaphore_signal(barrier, inc=1, device_id=peer, device_id_type=MESH)
+    loads[0].wait()
     slot_row = bp_ref[...] - (seq * 128 - 64)
 
     def slots(first, count):
@@ -147,13 +149,15 @@
     ones = slots(0, bs.shape[0]).astype(F32)
     count = jnp.maximum(jnp.sum(ones, axis=1, keepdims=True), 1.0)
     onehot[...] = ones.astype(BF)
-    load.wait()
+    loads[1].wait()
 
     @pl.loop(0, 4)
     def _(i):
         cols = pl.ds(pl.multiple_of(i * 256, 256), 256)
         pooled[:, cols] = (dot(onehot[...], bs[:, cols]) / count).astype(BF)
 
+    for copy in loads[2:]:
+        copy.wait()
     pl.semaphore_wait(barrier, len(peers))
 
     phase_start(wc, 0, 1, (1, 2, 3))
@@ -210,14 +214,16 @@
     for core in (0, 1):
         send(edge, e1b.at[1 - k], es.at[2 + core], er.at[3 - k], (near * 2 + core, z))
     arrive(wbuf.at[1 - k], es.at[1], er.at[1])
-    arrive(e1b.at[0], es.at[2], er.at[2])
-    arrive(e1b.at[1], es.at[3], er.at[3])
-    xbuf[0:64, :] = wbuf[0, 64:128, :] + e1b[0]
     xbuf[64:192, :] = wbuf[0, 128:256, :] + wbuf[1, 0:128, :]
-    xbuf[192:256, :] = wbuf[1, 128:192, :] + e1b[1]
     relay_wait(wp, 1)
-    phase_wait(wp, 2, 1, (1, 2, 3))
-    phase_start(wp, 2, 2, (1, 3))
+
+    def first_late():
+        arrive(e1b.at[0], es.at[2], er.at[2])
+        arrive(e1b.at[1], es.at[3], er.at[3])
+        xbuf[0:64, :] = wbuf[0, 64:128, :] + e1b[0]
+        xbuf[192:256, :] = wbuf[1, 128:192, :] + e1b[1]
+        phase_wait(wp, 2, 1, (1, 2, 3))
+        phase_start(wp, 2, 2, (1, 3))
 
     def chunk_of(g, j):
         r, n = GROUPS[g]
@@ -239,9 +245,9 @@
         rsend[w, slot, rows] = value.astype(BF)
         send(rsend.at[w, slot, rows], rrecv.at[w, slot, rows], rss.at[w, slot, p], rsr.at[w, slot, p], target)
 
-    def reduce_depth(w, part, hook, result):
-        def share(side, away):
-            return part(wrap(z + away if side == 0 else z - away, DEPTH))
+    def reduce_depth(w, part, late, hook, result):
+        def share(side, away, rows=slice(0, ROWS)):
+            return part(wrap(z + away if side == 0 else z - away, DEPTH), rows)
 
         def strips(term):
             return [term[p * STRIP : (p + 1) * STRIP] for p in range(PARTS)]
@@ -252,30 +258,31 @@
             for side, main in mains.items():
                 give(w, main_slot(side, m), p, main, far[side])
             for side in range(2):
-                give(w, side_slot(side, m), p, sides[side][p], near[side])
-
-        first_main = strips(share(0, 2 * HOPS))
-        first_sides = [strips(share(side, 2 * HOPS - 1)) for side in range(2)]
-        for p in range(PARTS):
-            give_step(0, p, {0: first_main[p]}, first_sides)
+                give(w, side_slot(side, m), p, sides[side], near[side])
+
+        for p in ORDER:
+            if p == ORDER[2]:
+                late()
+            rows = slice(p * STRIP, (p + 1) * STRIP)
+            give_step(0, p, {0: share(0, 2 * HOPS, rows)}, [share(side, 2 * HOPS - 1, rows) for side in range(2)])
         for m in range(HOPS):
             last = m + 1 == HOPS
             away = 2 * (HOPS - 1 - m)
             terms = [strips(share(side, away)) for side in range(1 if last else 2)]
             sides = None if last else [strips(share(side, away - 1)) for side in range(2)]
-            for p in range(PARTS):
+            for p in ORDER:
                 sums = [received(w, side_slot(side, m), p) for side in range(2)]
                 for side in range(2 if m else 1):
                     sums[side] = sums[side] + received(w, main_slot(side, m), p)
                 if last:
                     result(slice(p * STRIP, (p + 1) * STRIP), terms[0][p] + sums[0] + sums[1])
                 else:
-                    give_step(m + 1, p, {side: terms[side][p] + sums[side] for side in range(2)}, sides)
+                    give_step(m + 1, p, {side: terms[side][p] + sums[side] for side in range(2)}, [sides[0][p], sides[1][p]])
             hook(m)
 
-    def first_part(j):
+    def first_part(j, rows):
         w = chunk_of(1, j)
-        return dot(xbuf[:, 0:128], w[:, 0:128]) + dot(xbuf[:, 128:256], w[:, 128:256])
+        return dot(xbuf[rows, 0:128], w[:, 0:128]) + dot(xbuf[rows, 128:256], w[:, 128:256])
 
     def first_hook(u):
         if u == 1:
@@ -298,7 +305,7 @@
         latent[rows] = ag[z, rows]
         pass_on(0, rows.start // STRIP)
 
-    reduce_depth(0, first_part, first_hook, first_result)
+    reduce_depth(0, first_part, first_late, first_hook, first_result)
 
     def project(js, fresh):
         pieces, weights = [], []
@@ -330,8 +337,8 @@
         if m + 1 < HOPS:
             mains.append((main_slot(1, m + 1), wrap(z + 2 * (m + 1), DEPTH)))
         sides = [(side_slot(0, m), wrap(z - 1 - 2 * m, DEPTH)), (side_slot(1, m), wrap(z + 1 + 2 * m, DEPTH))]
-        for p in range(PARTS):
-            if m + 1 == HOPS and p == PARTS - 1:
+        for p in ORDER:
+            if m + 1 == HOPS and p == ORDER[-1]:
                 for slot, j in sides:
                     for strip in range(PARTS):
                         take(j, slot, strip)
@@ -340,7 +347,7 @@
                 take(j, slot, p)
             if m + 1 < HOPS:
                 pass_on(m + 1, p)
-            if p == 0 and held is not None:
+            if p == ORDER[0] and held is not None:
                 project(held, False)
         if m + 1 < HOPS:
             for slot, j in sides:
@@ -443,14 +450,14 @@
     send(att.at[k], att.at[k], es.at[5], er.at[5], partner)
     arrive(att.at[1 - k], es.at[5], er.at[5])
 
-    def second_part(j):
+    def second_part(j, rows):
         w = chunk_of(3, j)
-        return dot(att[0], w[:, 0:128]) + dot(att[1], w[:, 128:256])
+        return dot(att[0, rows], w[:, 0:128]) + dot(att[1, rows], w[:, 128:256])
 
     def second_result(rows, value):
         fin_s[rows] = (latent[rows].astype(F32) + value).astype(BF)
 
-    reduce_depth(1, second_part, lambda m: None, second_result)
+    reduce_depth(1, second_part, lambda: None, lambda m: None, second_result)
     theirs = fin_s.at[pl.ds(pl.multiple_of((1 - k) * 128, 128), 128), :]
     send(theirs, fin_r, es.at[6], er.at[6], partner)
     mine = pl.ds(pl.multiple_of(k * 128, 128), 128)
@@ -473,10 +480,12 @@
     return pl.pallas_call(
         kernel,
         out_shape=jax.ShapeDtypeStruct((128, 256), BF),
-        in_specs=[pl.BlockSpec(memory_space=pl.ANY)] + [vmem] * 10,
+        in_specs=[pl.BlockSpec(memory_space=pl.ANY)] * 11,
         out_specs=vmem,
         scratch_shapes=[
             pltpu.VMEM((bytes_here, width), BF),
+            pltpu.VMEM((1, bytes_here), jnp.int32),
+            pltpu.VMEM((2 * DEPTH, HEAD_DIM), F32),
             pltpu.VMEM((SIDE, SIDE, PACKED, 256), BF),
             pltpu.VMEM((SIDE, SIDE, 2, 3, 32, 256), BF),
             pltpu.VMEM((ROWS, width), BF),
@@ -498,7 +507,7 @@
             pltpu.VMEM(block, BF),
             pltpu.VMEM(block, BF),
             pltpu.VMEM((128, HEAD_DIM), BF),
-            dma,
+            dma((13,)),
             dma((groups, 2, 3)),
             dma((groups, 2, 3)),
             dma((groups, 2, 3)),

time: 122 us -> 120 us (0.984)
  Pallas kernels: 121 us -> 118 us
    pallas_call x1, Pallas kernels: 121 us -> 118 us  [per_device(): pl.pallas_call(kernel, out_shape=jax.ShapeDtypeStruct((128, 256), BF), in...]
where the time goes in v5:
time: 120 us; the launch traced here: 119 us
  Pallas kernels  118 us (98%)
  local copies, waits for them, and re-layouts  1.47 us (1%)
    pallas_call x1, Pallas kernels, per_device(): pl.pallas_call(kernel, out_shape=jax.ShapeDtypeStruct((128, 256), BF), in...  118 us

profile of v5, /device:TPU:1, one launch (start us, length us, event | category | flops | bytes accessed | tf_op | source)
XLA Modules:
  0.0 119.4 jit_solution(3094756122771258433)
XLA Ops:
  0.0 117.9 %patches.1 = bf16[128,256]{1,0:T(8,128)(2,1)} custom-call(bf16[1024,1024]{1,0:T(8,128)(2,1)} %bs_in.1, s32[1,1024]{1,0:T(1,128)} %bitcast.3, bf16[32,256]{1,0:T(8,128)(2,1)} %cq.1, bf16[32,256]{1,0:T(8,128)(2,1)} %ck.1, bf16[32,256]{1,0:T(8,128)(2,1)} %cv.1, bf16[256,128]{1,0:T(8,128)(2,1)} %co.1, f32[32,128]{1,0:T(8,128)} %bitcast.2, bf16[128,256]{1,0:T(8,128)(2,1)} %lq.1, ...), custom_call_target="tpu_custom_call" | custom-call | tf_op jit(solution)/shard_map/patches/pallas_call | solution.py:480
  117.9 1.5 %copy.13 = bf16[128,256]{1,0:T(8,128)(2,1)} copy(bf16[128,256]{1,0:T(8,128)(2,1)} %patches.1) | data formatting | bytes 131072

commit v6 on v5

--- a/solution.py
+++ b/solution.py
@@ -43,7 +43,7 @@
     bs_in, bp_in, cq, ck, cv, co, gain_in, lq, lk, lv, lo,
     out_ref,
     bs, bp_ref, gain, wp, wc, pooled, onehot, wbuf, e1b, xbuf, rsend, rrecv, ag, acc, sq, e2, qs, kvb, oacc, lacc, att, latent, fin_s, fin_r,
-    bs_sem, p1s, p1r, p2s, p2r, rls, rlr, rss, rsr, ags, agr, es, er, kvs, kvr,
+    bs_sem, p1s, p1r, p2s, p2r, rls, rlr, rss, rsr, ags, agr, es, er, kvs, kvr, wcs, wcr,
 ):
     seq, z = lax.axis_index("seq"), lax.axis_index("tensor")
     k, c = lax.rem(seq, 2), lax.div(seq, 2)
@@ -160,22 +160,35 @@
         copy.wait()
     pl.semaphore_wait(barrier, len(peers))
 
-    phase_start(wc, 0, 1, (1, 2, 3))
-    phase_start(wp, 1, 1, (1, 2, 3))
+    def wc_piece(half, q, d):
+        px, py = (wrap(x - q, SIDE), wrap(y - d, SIDE)) if half == 0 else (wrap(x - d, SIDE), wrap(y - q, SIDE))
+        return wc.at[px, py, k, :, pl.ds(*span(0, half)), :]
+
+    def wc_on(q):
+        for half in range(2):
+            held = wc_piece(half, q, 0)
+            for d in (2, 1, 3):
+                send(held, held, wcs.at[half, d - 1, q], wcr.at[half, d - 1, q], along(half, 2, d))
+
+    phase_start(wc, 0, 1, (1, 3, 2))
+    wc_on(0)
+    phase_start(wp, 1, 1, (1, 3, 2))
 
     def hand_over(half, d):
         held = piece(wc, half, 2, -d, *span(0, half))
         send(held, held, es.at[7 + 4 * half + d], er.at[7 + 4 * half + d], partner)
 
-    phase_wait(wc, 0, 1, (1, 2, 3))
-    phase_start(wc, 0, 2, (1, 3, 2))
+    for d in (1, 3, 2):
+        phase_wait(wc, 0, 1, (d,))
+        wc_on(d)
     for half in range(2):
         hand_over(half, 0)
     phase_wait(wp, 1, 1, (1, 2, 3))
     phase_start(wp, 1, 2, (1, 3))
     for d in (1, 3, 2):
-        phase_wait(wc, 0, 2, (d,))
-        for half in range(2):
+        for half in range(2):
+            for q in range(SIDE):
+                arrive(wc_piece(half, q, d), wcs.at[half, d - 1, q], wcr.at[half, d - 1, q])
             hand_over(half, d)
     relay_start(wp, 1)
     for half in range(2):
@@ -522,6 +535,8 @@
             dma((15,)),
             dma((2, SIDE, SIDE)),
             dma((2, SIDE, SIDE)),
+            dma((2, SIDE - 1, SIDE)),
+            dma((2, SIDE - 1, SIDE)),
         ],
         compiler_params=pltpu.CompilerParams(
             collective_id=0, has_side_effects=True, vmem_limit_bytes=60 * 1024 * 1024

time: 120 us -> 119 us (level)
  no operation moved by 1% of the time
where the time goes in v6:
time: 119 us
  Pallas kernels  118 us (99%)
  local copies, waits for them, and re-layouts  1.47 us (1%)
    pallas_call x1, Pallas kernels, per_device(): pl.pallas_call(kernel, out_shape=jax.ShapeDtypeStruct((128, 256), BF), in...  118 us

profile of v6, /device:TPU:1, one launch (start us, length us, event | category | flops | bytes accessed | tf_op | source)
XLA Modules:
  0.0 119.2 jit_solution(2689588383935916602)
XLA Ops:
  0.0 117.7 %patches.1 = bf16[128,256]{1,0:T(8,128)(2,1)} custom-call(bf16[1024,1024]{1,0:T(8,128)(2,1)} %bs_in.1, s32[1,1024]{1,0:T(1,128)} %bitcast.3, bf16[32,256]{1,0:T(8,128)(2,1)} %cq.1, bf16[32,256]{1,0:T(8,128)(2,1)} %ck.1, bf16[32,256]{1,0:T(8,128)(2,1)} %cv.1, bf16[256,128]{1,0:T(8,128)(2,1)} %co.1, f32[32,128]{1,0:T(8,128)} %bitcast.2, bf16[128,256]{1,0:T(8,128)(2,1)} %lq.1, ...), custom_call_target="tpu_custom_call" | custom-call | tf_op jit(solution)/shard_map/patches/pallas_call | solution.py:493
  117.7 1.5 %copy.13 = bf16[128,256]{1,0:T(8,128)(2,1)} copy(bf16[128,256]{1,0:T(8,128)(2,1)} %patches.1) | data formatting | bytes 131072
